TPU v7x, 256 devices: a whole 4x4x8 slice. The times are simulated.
256 devices in a mesh: req: 32 (over z, y), seq: 8 (over x, core).
Axes of the slice: x: 4, y: 4, z: 8, core: 2. Of those that a mesh axis runs over, the one named last changes fastest.
Arguments:
- tokens: bfloat16 [32, 4096, 2560], P('req', 'seq'), may hold values from -6 to 6
- mix_weight: bfloat16 [2560, 2816], P(('req', 'seq')), may hold values from -0.125 to 0.125
- step_weight: bfloat16 [2560, 40], P(('req', 'seq')), may hold values from -0.125 to 0.125
- conv_weight: float32 [4, 2816], replicated, may hold values from -3 to 3
- conv_bias: float32 [2816], replicated, may hold values from -3 to 3
- step_bias: float32 [40], replicated, may hold values from -5 to -3
- decay_rate: float32 [40], replicated, may hold values from 0.00048828125 to 1
- skip_gain: float32 [40], replicated, may hold values from 0.5 to 2
- norm_gain: float32 [2560], replicated, may hold values from 0.1 to 1.9
- prompt_len: int32 [32], replicated, may hold values from 1024 to 4096, as said below
- prompt_start: int32 [32], replicated, may hold values from 0 to 3072, as said below
- deal: int32 [32], replicated, may hold values from 0 to 31, as said below
Outputs:
- result: bfloat16 [32, 4096, 2560], P('req', 'seq')
- final_state: float32 [32, 40, 64, 128], P('req', 'seq')
Inputs may be any that keep to these rules, and one draw needn't show every extreme that they name: `prompt_len`: one prompt has exactly 4096 positions and one exactly a quarter of 4096. prompt_start plus prompt_len is at most 4096 for every request. `deal`: a permutation of the requests; some slot s holds request (s + 16) modulo 32.
All inputs are finite; a program needn't handle non-finite values.
Results may differ from a plain program's by a relative error of at most 0.0035.
Values may be sent and summed in bfloat16 or wider, within the bound.
A program may use at most 128 MiB of HBM per device.

v0:
```python
import jax
import jax.numpy as jnp
from jax import lax
from jax.sharding import PartitionSpec as P

GROUP = 256
EPS = 1e-05


def passed_along(block, axis, distance):
    devices = range(lax.axis_size(axis))
    route = [(i - distance, i) for i in devices if i - distance in devices]
    return lax.ppermute(block, axis, route)


def carried_in(part, axis, combine, identity):
    place = lax.axis_index(axis)
    gathered = jax.tree.map(lambda a: lax.all_gather(a, axis), part)
    state = jax.tree.map(lambda a, e: jnp.zeros_like(a) + jnp.asarray(e, a.dtype), part, identity)

    def one(step, state):
        return combine(
            state, jax.tree.map(lambda a: lax.dynamic_index_in_dim(a, step, 0, False), gathered)
        )

    return lax.fori_loop(0, place, one, state)


def broadcast(x, axis, root):
    mine = lax.axis_index(axis) == root
    return lax.psum(jnp.where(mine, x, jnp.zeros_like(x)), axis)


def on_device(
    tokens,
    mix_weight,
    step_weight,
    conv_weight,
    conv_bias,
    step_bias,
    decay_rate,
    skip_gain,
    norm_gain,
    prompt_len,
    prompt_start,
    deal,
):
    seq_count = lax.axis_size("seq")
    seq_index = lax.axis_index("seq")
    req_index = lax.axis_index("req")
    rows = tokens[0]
    span = rows.shape[0]
    total_reqs = deal.shape[0]
    slots = jnp.arange(total_reqs, dtype=jnp.int32)
    request = jnp.sum(jnp.where(slots == req_index, deal, 0))
    length = jnp.sum(jnp.where(slots == request, prompt_len, 0))
    start = jnp.sum(jnp.where(slots == request, prompt_start, 0))
    place = seq_index * span + jnp.arange(span, dtype=jnp.int32)
    valid = ((place >= start) & (place < start + length)).astype(jnp.float32)
    whole_mix, whole_step = (
        lax.all_gather(mix_weight, ("req", "seq"), axis=0, tiled=True),
        lax.all_gather(step_weight, ("req", "seq"), axis=0, tiled=True),
    )
    mixed = jnp.dot(rows, whole_mix, preferred_element_type=jnp.float32)
    raw_step = jnp.dot(rows, whole_step, preferred_element_type=jnp.float32)
    mixed = (mixed * valid[:, None]).astype(jnp.bfloat16)
    taps = conv_weight.shape[0]
    edge = passed_along(mixed[span - (taps - 1) :], "seq", 1)
    padded = jnp.concatenate([edge, mixed], axis=0)
    conv_sum = jnp.zeros(mixed.shape, jnp.float32) + conv_bias[None, :]
    for offset in range(taps):
        conv_sum = conv_sum + conv_weight[offset][None, :] * padded[offset : offset + span].astype(
            jnp.float32
        )
    convolved = jax.nn.silu(conv_sum).astype(jnp.bfloat16)
    heads = decay_rate.shape[0]
    inner = norm_gain.shape[0]
    head_dim = inner // heads
    nstate = (mixed.shape[1] - inner) // 2
    blocks = span // GROUP
    inputs = convolved[:, :inner].reshape(span, heads, head_dim)
    mixed_b = convolved[:, inner : inner + nstate]
    mixed_c = convolved[:, inner + nstate :]
    step_size = jax.nn.softplus(raw_step + step_bias[None, :]) * valid[:, None]
    pieces = (
        inputs.reshape(blocks, GROUP, heads, head_dim),
        mixed_b.reshape(blocks, GROUP, nstate),
        mixed_c.reshape(blocks, GROUP, nstate),
        step_size.reshape(blocks, GROUP, heads),
    )

    def local_group(block):
        part_in, part_b, part_c, part_step = block
        cum_decay = jnp.cumsum(-part_step * decay_rate[None, :], axis=0)
        places = jnp.arange(GROUP, dtype=jnp.int32)
        causal = places[:, None] >= places[None, :]
        spread = cum_decay[:, None, :] - cum_decay[None, :, :]
        spread = jnp.where(causal[:, :, None], spread, -1e30)
        scores = jnp.einsum("qn,kn->qk", part_c, part_b, preferred_element_type=jnp.float32)
        mixing = (jnp.exp(spread) * scores[:, :, None] * part_step[None, :, :]).astype(jnp.bfloat16)
        inner_out = jnp.einsum("qkh,khp->qhp", mixing, part_in, preferred_element_type=jnp.float32)
        to_end = jnp.exp(cum_decay[-1][None, :] - cum_decay) * part_step
        scaled = (to_end[:, :, None] * part_in.astype(jnp.float32)).astype(jnp.bfloat16)
        local = jnp.einsum("khp,kn->hpn", scaled, part_b, preferred_element_type=jnp.float32)
        return (inner_out, cum_decay, local)

    inner_out, cum_decay, group_state = lax.map(local_group, pieces)
    totals = cum_decay[:, -1, :]

    def advance(carry, item):
        group_total, group_local = item
        return (jnp.exp(group_total)[:, None, None] * carry + group_local, carry)

    dev_state, entry_zero = lax.scan(
        advance, jnp.zeros((heads, head_dim, nstate), jnp.float32), (totals, group_state)
    )
    before = jnp.cumsum(totals, axis=0) - totals
    dev_decay = jnp.exp(jnp.sum(totals, axis=0))

    def chain(earlier, later):
        return (earlier[0] * later[0], later[0][:, None, None] * earlier[1] + later[1])

    incoming_decay, incoming = carried_in(
        (dev_decay, dev_state), "seq", chain, (jnp.ones_like(dev_decay), jnp.zeros_like(dev_state))
    )
    entry = entry_zero + jnp.exp(before)[:, :, None, None] * incoming[None]
    carried = jnp.einsum(
        "cqn,chpn->cqhp", pieces[2].astype(jnp.float32), entry, precision=lax.Precision.HIGHEST
    )
    carried = carried * jnp.exp(cum_decay)[:, :, :, None]
    outputs = (inner_out + carried).reshape(span, heads, head_dim) + skip_gain[
        None, :, None
    ] * inputs.astype(jnp.float32)
    flat = outputs.reshape(span, inner)
    factor = lax.rsqrt(jnp.mean(flat * flat, axis=1, keepdims=True) + EPS)
    result = (flat * factor * norm_gain[None, :] * valid[:, None]).astype(jnp.bfloat16)[None]
    share = heads // seq_count
    leaving = dev_decay[:, None, None] * incoming + dev_state
    last_state = broadcast(leaving, "seq", seq_count - 1)
    own_state = lax.dynamic_slice_in_dim(last_state, seq_index * share, share, 0)[None]
    wanted = jnp.sum(jnp.where(deal == req_index, slots, 0))
    piece = lax.all_gather(own_state, "req", axis=0, tiled=True)
    count = piece.shape[0]
    chosen = jnp.arange(count, dtype=jnp.int32) == wanted
    final_state = jnp.zeros_like(own_state) + jnp.sum(
        jnp.where(chosen[:, None, None, None], piece, 0.0), axis=0, keepdims=True
    )
    return (result, final_state)


def solution(mesh):
    return jax.shard_map(
        on_device,
        mesh=mesh,
        in_specs=(
            P("req", "seq", None),
            P(("req", "seq"), None),
            P(("req", "seq"), None),
            P(),
            P(),
            P(),
            P(),
            P(),
            P(),
            P(),
            P(),
            P(),
        ),
        out_specs=(P("req", "seq", None), P("req", "seq", None, None)),
        check_vma=False,
    )
```

profile of v0, /device:TPU:2, one launch (start us, length us, event | category | flops | bytes accessed | tf_op | source)
XLA Modules:
  0.0 482.0 jit_solution(1051136293453293092)
XLA Ops:
  7.2 0.7 all-gather.13.cloned.1.call-update
  8.0 70.5 %all-gather.4 = bf16[256,10,40]{2,1,0:T(8,128)(2,1)} all-gather(bf16[1,10,40]{2,1,0:T(8,128)(2,1)} %bitcast.158), channel_id=1, replica_groups=mesh['req'=32,'seq'=8] {'req','seq'}, dimensions={0}, use_global_device_ids=true | all-gather | bytes 205600 | tf_op jit(solution)/shard_map/all_gather | solution.py:62
  78.4 1.5 reshape.119
  80.0 1.3 fusion.54
  81.3 1.9 fusion.51
  83.2 2.0 fusion.52
  86.5 0.6 fusion.50
  87.2 1.6 fusion.44
  88.7 60.2 %all-gather.13.cloned.1.call-done = bf16[256,10,2816]{2,1,0:T(8,128)(2,1)} async-done(((bf16[1,10,2816]{2,1,0:T(8,128)(2,1)}), bf16[256,10,2816]{2,1,0:T(8,128)(2,1)}) %all-gather.13.cloned.1.call-update) | async-done | bytes 14417936 | tf_op jit(solution)/shard_map/all_gather | solution.py:61
  149.0 25.3 %reshape.117 = bf16[2560,2816]{1,0:T(8,128)(2,1)} reshape(bf16[256,10,2816]{2,1,0:T(8,128)(2,1)} %all-gather.13.cloned.1.call-done) | data formatting | bytes 28835840
  174.2 11.5 %multiply_convert_fusion.6 = bf16[512,2816]{1,0:T(8,128)(2,1)S(1)} fusion(bf16[2560,2816]{1,0:T(8,128)(2,1)} %reshape.117, f32[512]{0:T(512)S(1)} %fusion.50, bf16[1,512,2560]{2,1,0:T(8,128)(2,1)S(1)} %copy-done), kind=kOutput, calls=%fused_computation.48 | convolution fusion | flops 7384858624 | bytes 19924992 | tf_op jit(solution)/shard_map/dot_general | solution.py:64
  185.8 1.6 copy-done.7
  187.4 2.3 collective-permute-start
  189.7 0.1 slice_reduce_fusion.7
  189.9 2.6 collective-permute-done
  192.5 7.8 %multiply_convert_fusion.5 = bf16[512,2816]{1,0:T(8,128)(2,1)S(1)} fusion(bf16[512,2816]{1,0:T(8,128)(2,1)} %copy-done.7, bf16[3,2816]{1,0:T(4,128)(2,1)S(1)} %collective-permute-done, f32[2816]{0:T(1024)S(1)} %get-tuple-element.187, f32[2816]{0:T(1024)S(1)} %get-tuple-element.188, f32[2816]{0:T(1024)S(1)} %get-tuple-element.186, ...), kind=kLoop, calls=%fused_computation.47 | loop fusion | flops 37486592 | bytes 5840384 | tf_op jit(solution)/shard_map/convert_element_type | solution.py:75
  200.3 1.5 copy-done.5
  201.8 1.7 slice.64
  203.5 7.5 %reshape.124 = bf16[2,256,40,64]{3,2,1,0:T(8,128)(2,1)} reshape(bf16[512,2560]{1,0:T(8,128)(2,1)} %slice.64) | data formatting | bytes 5242880 | tf_op jit(solution)/shard_map/reshape;reshape | solution.py:86
  211.0 6.4 %copy.40 = bf16[2,256,40,64]{1,3,2,0:T(8,128)(2,1)} copy(bf16[2,256,40,64]{3,2,1,0:T(8,128)(2,1)} %reshape.124) | data formatting | bytes 5242880 | tf_op jit(solution)/shard_map/while | solution.py:107
  217.5 1.8 broadcast.58.clone
  219.3 17.0 %while.39 = (s32[]{:T(128)}, f32[2,256,40,64]{1,3,2,0:T(8,128)}, f32[2,256,40]{1,2,0:T(8,128)S(1)}, f32[2,40,64,128]{3,2,1,0:T(8,128)}, bf16[2,256,40,64]{1,3,2,...) while((s32[]{:T(128)}, f32[2,256,40,64]{1,3,2,0:T(8,128)}, ...), condition=%wide.region_6.7_spmd, body=%wide.region_3.6_spmd.sunk | while | flops 536604800 | bytes 18677688 | solution.py:107
  219.4 0.6 reduce-window.12
  220.0 0.2 slice_reduce_fusion.10
  220.3 0.2 fusion.74
  220.5 5.3 %bitcast_dynamic-update-slice_fusion.4 = f32[2,256,40,64]{1,3,2,0:T(8,128)} fusion(f32[2,256,40,64]{1,3,2,0:T(8,128)} %get-tuple-element.363, s32[]{:T(128)} %get-tuple-element.362, f32[256,40]{0,1:T(8,128)S(1)} %bitcast.155, f32[256,256]{1,0:T(8,128)S(1)} %fusion.74, f32[256,40]{0,1:T(8,128)S(1)} %bitcast_bitcast_fusion.3, ...), kind=kOutput, calls=%fused_computation.15.clone.1 | convolution fusion | flops 348651520 | bytes 4383744 | tf_op jit(solution)/shard_map/while/body/eval_jaxpr/qkh,khp->qhp/dot_general | solution.py:101
  225.8 0.2 slice_reduce_fusion.11
  226.0 0.1 exponential_multiply_fusion.2
  226.1 1.6 fusion.76
  227.9 0.6 reduce-window.12
  228.5 0.2 slice_reduce_fusion.10
  228.8 0.2 fusion.74
  229.0 5.3 %bitcast_dynamic-update-slice_fusion.4 = f32[2,256,40,64]{1,3,2,0:T(8,128)} fusion(f32[2,256,40,64]{1,3,2,0:T(8,128)} %get-tuple-element.363, s32[]{:T(128)} %get-tuple-element.362, f32[256,40]{0,1:T(8,128)S(1)} %bitcast.155, f32[256,256]{1,0:T(8,128)S(1)} %fusion.74, f32[256,40]{0,1:T(8,128)S(1)} %bitcast_bitcast_fusion.3, ...), kind=kOutput, calls=%fused_computation.15.clone.1 | convolution fusion | flops 348651520 | bytes 4383744 | tf_op jit(solution)/shard_map/while/body/eval_jaxpr/qkh,khp->qhp/dot_general | solution.py:101
  234.3 0.2 slice_reduce_fusion.11
  234.6 1.6 fusion.76
  236.3 0.2 slice_reduce_fusion.2
  236.5 1.9 broadcast.58
  238.3 5.6 %while.41 = (s32[]{:T(128)}, f32[40,64,128]{2,1,0:T(8,128)S(1)}, f32[2,40,64,128]{3,2,1,0:T(8,128)}, f32[2,40]{1,0:T(2,128)S(1)}, f32[2,40,64,128]{3,2,1,0:T(8,128)}, /*index=5*/s32[]{:T(128)}, s32[]{:T(128)}) while((s32[]{:T(128)}, f32[40,64,128]{2,1,0:T(8,128)S(1)}, f32[2,40,64,128]{3,2,1,0:T(8,128)}, f32[2,40]{1,0:T(2,128)S(1)}, ...), condition=%wide.region_8.9_spmd.clone, body=%wide.region_7.8_spmd.clone.sunk | while | flops 1310723 | bytes 6554688 | solution.py:114
  238.3 1.3 bitcast_dynamic-update-slice_fusion.5
  239.6 1.5 bitcast_add_fusion.5
  241.2 1.2 bitcast_dynamic-update-slice_fusion.5
  242.4 1.5 bitcast_add_fusion.5
  244.0 1.0 copy-done.2
  245.1 0.6 dynamic-slice
  246.5 0.1 fusion.56
  246.6 10.0 %all-reduce = f32[320]{0:T(512)S(1)} all-reduce(f32[320]{0:T(512)S(1)} %get-tuple-element.232), channel_id=2, replica_groups=mesh['req'=32,'seq'=8] {'seq'}, use_global_device_ids=true, to_apply=%add | all-reduce | flops 320 | bytes 2560
  256.6 46.0 %all-gather.9.cloned.1.call-done = f32[320,64,128]{2,1,0:T(8,128)} async-done(((f32[40,64,128]{2,1,0:T(8,128)}), f32[320,64,128]{2,1,0:T(8,128)}) %all-gather.9.cloned.1.call-update) | async-done | bytes 10485776 | tf_op jit(solution)/shard_map/all_gather | solution.py:18
  302.6 0.1 broadcast.59
  302.8 3.3 while.40
  302.8 1.7 bitcast_add_fusion.4
  304.5 1.6 bitcast_add_fusion.4
  306.2 1.3 add_select_fusion
  307.4 0.3 all-gather.11.cloned.1.call-start
  307.7 74.1 %all-reduce.3.cloned.1.call-done = f32[40,64,128]{2,1,0:T(8,128)} async-done(((f32[40,64,128]{2,1,0:T(8,128)}), f32[40,64,128]{2,1,0:T(8,128)}) %all-reduce.3.cloned.1.call-update) | async-done | bytes 1310736 | tf_op jit(solution)/shard_map/psum | solution.py:31
  381.8 1.6 constant_dynamic-slice_fusion.2
  383.6 0.6 iota_compare_fusion.1
  384.3 8.0 %multiply_add_fusion.1 = f32[2,256,40,64]{1,3,2,0:T(8,128)} fusion(f32[2,256,40,64]{1,3,2,0:T(8,128)} %get-tuple-element.123, f32[2,256,40]{1,2,0:T(8,128)S(1)} %exp.56, bf16[2,256,128,1]{2,1,3,0:T(8,128)(2,1)S(1)} %bitcast.154, f32[2,40,64,128]{3,2,1,0:T(8,128)} %get-tuple-element.126, f32[40,64,128]{2,1,0:T(8,128)S(1)} %get-tuple-element.128, ...), kind=kOutput, calls=%fused_computation.53 | convolution fusion | flops 2017198080 | bytes 14631232 | tf_op jit(solution)/shard_map/cqn,chpn->cqhp/dot_general | solution.py:127
  392.4 8.6 %copy.47 = f32[2,256,40,64]{3,2,1,0:T(8,128)} copy(f32[2,256,40,64]{1,3,2,0:T(8,128)} %multiply_add_fusion.1) | data formatting | bytes 10485760 | tf_op jit(solution)/shard_map/reshape | solution.py:131
  401.0 9.6 %reshape.125 = f32[512,2560]{1,0:T(8,128)} reshape(f32[2,256,40,64]{3,2,1,0:T(8,128)} %copy.47) | data formatting | bytes 10485760 | tf_op jit(solution)/shard_map/reshape | solution.py:131
  410.6 4.4 multiply_reduce_fusion
  415.0 0.4 copy-done.4
  415.4 4.7 fusion.30
  420.1 51.5 %all-gather.11.cloned.1.call-done = f32[160,64,128]{2,1,0:T(8,128)} async-done(((f32[5,64,128]{2,1,0:T(8,128)}), f32[160,64,128]{2,1,0:T(8,128)}) %all-gather.11.cloned.1.call-update) | async-done | bytes 5242896 | tf_op jit(solution)/shard_map/all_gather | solution.py:142
  471.6 3.9 select_reduce_fusion
  (67 shorter events, 1.4 us)
Async XLA Ops:
  7.2 80.0 %copy-start = (bf16[1,512,2560]{2,1,0:T(8,128)(2,1)S(1)}, bf16[1,512,2560]{2,1,0:T(8,128)(2,1)}, u32[]{:S(2)}) copy-start(bf16[1,512,2560]{2,1,0:T(8,128)(2,1)} %param.18) | copy-start | bytes 7864324
  7.2 141.8 %all-gather.13.cloned.1.call-start = ((), (), s32[]{:S(2)}) async-start(), calls=%async_computation.3 | async-start | bytes 23158784 | tf_op jit(solution)/shard_map/all_gather | solution.py:61
  7.9 294.7 %all-gather.9.cloned.1.call-start = ((), (), s32[]{:S(2)}) async-start(), calls=%async_computation.1 | async-start | bytes 11796480 | tf_op jit(solution)/shard_map/all_gather | solution.py:18
  174.2 15.5 %copy-start.8 = (f32[4,2816]{1,0:T(4,128)S(1)}, f32[4,2816]{1,0:T(4,128)}, u32[]{:S(2)}) copy-start(f32[4,2816]{1,0:T(4,128)} %param.21) | copy-start | bytes 135172
  174.2 18.2 %copy-start.10 = (f32[2816]{0:T(1024)S(1)}, f32[2816]{0:T(1024)}, u32[]{:S(2)}) copy-start(f32[2816]{0:T(1024)} %param.22) | copy-start | bytes 33796
  185.8 1.6 copy-start.7
  187.4 5.1 %collective-permute-start = (bf16[3,2816]{1,0:T(4,128)(2,1)S(1)}, bf16[3,2816]{1,0:T(4,128)(2,1)S(1)}, u32[]{:S(2)}, u32[]{:S(2)}) collective-permute-start(bf16[3,2816]{1,0:T(4,128)(2,1)S(1)} %slice.59), channel_id=1, source_target_pairs={{0,1},{1,2},{2,3},{3,4},{4,5},{5,6},{6,7},{8,9},{9,10},{10,11},{11... | collective-permute-start | bytes 50696 | tf_op jit(solution)/shard_map/ppermute | solution.py:13
  200.3 1.5 copy-start.5
  211.0 8.2 %copy-start.9 = (f32[40]{0:T(128)S(1)}, f32[40]{0:T(128)}, u32[]{:S(2)}) copy-start(f32[40]{0:T(128)} %param.24) | copy-start | bytes 484
  220.5 5.6 %copy-start.6 = (bf16[2,256,40,64]{1,3,2,0:T(8,128)(2,1)S(1)}, bf16[2,256,40,64]{1,3,2,0:T(8,128)(2,1)}, u32[]{:S(2)}) copy-start(bf16[2,256,40,64]{1,3,2,0:T(8,128)(2,1)} %get-tuple-element.377) | copy-start | bytes 7864324 | tf_op jit(solution)/shard_map/while
  229.0 5.6 %copy-start.6 = (bf16[2,256,40,64]{1,3,2,0:T(8,128)(2,1)S(1)}, bf16[2,256,40,64]{1,3,2,0:T(8,128)(2,1)}, u32[]{:S(2)}) copy-start(bf16[2,256,40,64]{1,3,2,0:T(8,128)(2,1)} %get-tuple-element.377) | copy-start | bytes 7864324 | tf_op jit(solution)/shard_map/while
  238.3 6.8 %copy-start.13 = (u32[256]{0:T(256)S(1)}, u32[256]{0:T(256)}, u32[]{:S(2)}) copy-start(u32[256]{0:T(256)} %constant.93) | copy-start | bytes 3076
  244.0 1.1 copy-start.2
  245.0 136.8 %all-reduce.3.cloned.1.call-start = ((), (), s32[]{:S(2)}) async-start(), calls=%async_computation | async-start | bytes 2621440 | tf_op jit(solution)/shard_map/psum | solution.py:31
  302.8 3.4 copy-start.3
  306.1 77.3 %copy-start.12 = (f32[40]{0:T(128)S(1)}, f32[40]{0:T(128)}, u32[]{:S(2)}) copy-start(f32[40]{0:T(128)} %param.25) | copy-start | bytes 484
  307.4 164.1 %all-gather.11.cloned.1.call-start = ((), (), s32[]{:S(2)}) async-start(), calls=%async_computation.2 | async-start | bytes 5406720 | tf_op jit(solution)/shard_map/all_gather | solution.py:142
  410.6 4.8 %copy-start.4 = (f32[512,2560]{1,0:T(8,128)S(1)}, f32[512,2560]{1,0:T(8,128)}, u32[]{:S(2)}) copy-start(f32[512,2560]{1,0:T(8,128)} %reshape.125) | copy-start | bytes 15728644
  410.6 4.8 %copy-start.11 = (f32[2560]{0:T(1024)S(1)}, f32[2560]{0:T(1024)}, u32[]{:S(2)}) copy-start(f32[2560]{0:T(1024)} %param.26) | copy-start | bytes 30724
  415.4 60.0 %copy-start.1 = (bf16[1,512,2560]{2,1,0:T(8,128)(2,1)S(1)}, bf16[1,512,2560]{2,1,0:T(8,128)(2,1)}, u32[]{:S(2)}) copy-start(bf16[1,512,2560]{2,1,0:T(8,128)(2,1)} %param.18) | copy-start | bytes 7864324
Sparse Core Ops, SparseCore 0:
  11.7 137.2 all-gather.12
  245.2 57.4 all-gather.8
  307.6 74.2 all-reduce.2
  384.9 86.6 all-gather.10
where the time goes:
time: 484 us; the launch traced here: 482 us
  waiting for transfers between devices  235 us (49%)
  blocking collectives  80.5 us (17%)
  local copies, waits for them, and re-layouts  72.7 us (15%)
  other arithmetic  39.5 us (8%)
  matrix products  35.3 us (7%)
  between operations  16 us (3%)
    psum x1, waiting for transfers between devices, broadcast(): return lax.psum(jnp.where(mine, x, jnp.zeros_like(x)), axis)  74.1 us
    all_gather x1, blocking collectives, on_device(): lax.all_gather(step_weight, ('req', 'seq'), axis=0, tiled=True)  70.5 us
    all_gather x1, waiting for transfers between devices, on_device(): lax.all_gather(mix_weight, ('req', 'seq'), axis=0, tiled=True)  60.2 us
    all_gather x1, waiting for transfers between devices, on_device(): piece = lax.all_gather(own_state, 'req', axis=0, tiled=True)  51.5 us
    all_gather x1, waiting for transfers between devices, carried_in(): gathered = jax.tree.map(lambda a: lax.all_gather(a, axis), part)  46 us
    unnamed x30, local copies, waits for them, and re-layouts  32 us
    reshape x2, local copies, waits for them, and re-layouts, on_device(): (inner_out + carried).reshape(span, heads, head_dim)  18.2 us
    dot_general x1, matrix products, on_device(): mixed = jnp.dot(rows, whole_mix, preferred_element_type=jnp.float32)  11.5 us
  transfers between devices with their start and end apart: 5, of which 5 were waited for; matrix products, arithmetic and copies ran while one was open for 10% of the time, Pallas kernels for 0%

commit v1 on v0

--- a/solution.py
+++ b/solution.py
@@ -5,6 +5,13 @@
 
 GROUP = 256
 EPS = 1e-05
+
+
+def all_by_exchange(shard, axis, dim):
+    count = lax.axis_size(axis)
+    blocks = jnp.stack([shard for _ in range(count)])
+    blocks = lax.all_to_all(blocks, axis, split_axis=0, concat_axis=0)
+    return jnp.concatenate(blocks, axis=dim)
 
 
 def passed_along(block, axis, distance):
@@ -58,7 +65,7 @@
     place = seq_index * span + jnp.arange(span, dtype=jnp.int32)
     valid = ((place >= start) & (place < start + length)).astype(jnp.float32)
     whole_mix, whole_step = (
-        lax.all_gather(mix_weight, ("req", "seq"), axis=0, tiled=True),
+        all_by_exchange(mix_weight, ("req", "seq"), 0),
         lax.all_gather(step_weight, ("req", "seq"), axis=0, tiled=True),
     )
     mixed = jnp.dot(rows, whole_mix, preferred_element_type=jnp.float32)

time: 484 us -> 932 us (1.93)
  blocking collectives: 80.5 us -> 565 us
  waiting for transfers between devices: 235 us -> 177 us
  starting transfers between devices: 2.72 us -> 18.4 us
    all_gather x1, blocking collectives: 70.5 us -> 554 us  [on_device(): lax.all_gather(step_weight, ('req', 'seq'), axis=0, tiled=True)]
    all_gather x1 -> x0, waiting for transfers between devices: 60.2 us -> none  [on_device(): lax.all_gather(mix_weight, ('req', 'seq'), axis=0, tiled=True)]
    unnamed x30 -> x39, local copies, waits for them, and re-layouts: 32 us -> 6.72 us
    reshape x0 -> x1, local copies, waits for them, and re-layouts: none -> 25.3 us  [all_by_exchange(): return jnp.concatenate(blocks, axis=dim)]
    all_to_all x0 -> x1, starting transfers between devices: none -> 15.6 us  [all_by_exchange(): blocks = lax.all_to_all(blocks, axis, split_axis=0, concat_axis=0)]
  transfers between devices with their start and end apart: 5 -> 5, of which waited for: 5 -> 4; matrix products, arithmetic and copies ran while one was open for 10% -> 5% of each run, Pallas kernels for 0% -> 0%
where the time goes in v1:
time: 932 us; the launch traced here: 930 us
  blocking collectives  565 us (61%)
  waiting for transfers between devices  177 us (19%)
  local copies, waits for them, and re-layouts  81.5 us (9%)
  other arithmetic  37.5 us (4%)
  matrix products  34.6 us (4%)
  starting transfers between devices  18.4 us (2%)
  between operations  16 us (2%)
    all_gather x1, blocking collectives, on_device(): lax.all_gather(step_weight, ('req', 'seq'), axis=0, tiled=True)  554 us
    psum x1, waiting for transfers between devices, broadcast(): return lax.psum(jnp.where(mine, x, jnp.zeros_like(x)), axis)  74.1 us
    all_gather x1, waiting for transfers between devices, on_device(): piece = lax.all_gather(own_state, 'req', axis=0, tiled=True)  51.6 us
    all_gather x1, waiting for transfers between devices, carried_in(): gathered = jax.tree.map(lambda a: lax.all_gather(a, axis), part)  46 us
    reshape x1, local copies, waits for them, and re-layouts, all_by_exchange(): return jnp.concatenate(blocks, axis=dim)  25.3 us
  transfers between devices with their start and end apart: 5, of which 4 were waited for; matrix products, arithmetic and copies ran while one was open for 5% of the time, Pallas kernels for 0%

profile of v1, /device:TPU:2, one launch (start us, length us, event | category | flops | bytes accessed | tf_op | source)
XLA Modules:
  0.0 930.2 jit_solution(17147431103008415207)
XLA Ops:
  7.2 8.9 stack.2
  16.1 15.6 %all-to-all-start = ((bf16[256,10,2816]{2,1,0:T(8,128)(2,1)}), bf16[256,10,2816]{2,1,0:T(8,128)(2,1)}, u32[]{:S(2)}, u32[]{:S(2)}) async-start(bf16[256,10,2816]{2,1,0:T(8,128)(2,1)} %stack.2), calls=%async_computation | async-start | bytes 46137344 | tf_op jit(solution)/shard_map/all_to_all | solution.py:13
  31.8 554.5 %all-gather.3 = bf16[256,10,40]{2,1,0:T(8,128)(2,1)} all-gather(bf16[1,10,40]{2,1,0:T(8,128)(2,1)S(1)} %bitcast.156), channel_id=1, replica_groups=mesh['req'=32,'seq'=8] {'req','seq'}, dimensions={0}, use_global_device_ids=true | all-gather | bytes 205600 | tf_op jit(solution)/shard_map/all_gather | solution.py:69
  586.2 1.5 reshape.123
  587.7 0.7 fusion.54
  588.4 1.3 fusion.51
  589.7 1.3 fusion.52
  592.3 0.6 fusion.50
  593.0 0.9 fusion.44
  593.9 25.3 %reshape.111 = bf16[2560,2816]{1,0:T(8,128)(2,1)} reshape(bf16[256,10,2816]{2,1,0:T(8,128)(2,1)} %all-to-all-done) | data formatting | bytes 28835840 | tf_op jit(solution)/shard_map/reshape | solution.py:14
  619.2 11.5 %multiply_convert_fusion.6 = bf16[512,2816]{1,0:T(8,128)(2,1)S(1)} fusion(bf16[2560,2816]{1,0:T(8,128)(2,1)} %reshape.111, f32[512]{0:T(512)S(1)} %fusion.50, bf16[1,512,2560]{2,1,0:T(8,128)(2,1)S(1)} %copy-done), kind=kOutput, calls=%fused_computation.48 | convolution fusion | flops 7384858624 | bytes 19924992 | tf_op jit(solution)/shard_map/dot_general | solution.py:71
  630.7 1.6 copy-done.7
  632.3 2.4 collective-permute-start
  634.8 0.1 slice_reduce_fusion.7
  635.0 5.3 collective-permute-done
  640.3 7.8 multiply_convert_fusion.5
  648.1 1.5 copy-done.5
  649.6 1.7 slice.64
  651.3 7.5 reshape.128
  658.9 6.4 copy.40
  665.3 1.8 broadcast.60.clone
  667.1 17.0 %while.39 = (s32[]{:T(128)}, f32[2,256,40,64]{1,3,2,0:T(8,128)}, f32[2,256,40]{1,2,0:T(8,128)S(1)}, f32[2,40,64,128]{3,2,1,0:T(8,128)}, bf16[2,256,40,64]{1,3,2,...) while((s32[]{:T(128)}, f32[2,256,40,64]{1,3,2,0:T(8,128)}, ...), condition=%wide.region_6.7_spmd, body=%wide.region_3.6_spmd.sunk | while | flops 536604800 | bytes 18677688 | solution.py:114
  667.2 0.6 reduce-window.12
  667.8 0.2 slice_reduce_fusion.10
  668.1 0.2 fusion.74
  668.3 5.3 bitcast_dynamic-update-slice_fusion.4
  673.6 0.2 slice_reduce_fusion.11
  673.8 0.1 exponential_multiply_fusion.2
  673.9 1.6 fusion.76
  675.7 0.6 reduce-window.12
  676.3 0.2 slice_reduce_fusion.10
  676.6 0.2 fusion.74
  676.8 5.3 bitcast_dynamic-update-slice_fusion.4
  682.1 0.2 slice_reduce_fusion.11
  682.4 1.6 fusion.76
  684.1 0.2 slice_reduce_fusion.2
  684.3 1.9 broadcast.60
  686.2 5.6 while.41
  686.2 1.3 bitcast_dynamic-update-slice_fusion.5
  687.5 1.5 bitcast_add_fusion.5
  689.0 1.2 bitcast_dynamic-update-slice_fusion.5
  690.2 1.5 bitcast_add_fusion.5
  691.8 1.0 copy-done.2
  692.9 0.6 dynamic-slice
  694.2 0.1 fusion.56
  694.3 10.3 %all-reduce = f32[320]{0:T(512)S(1)} all-reduce(f32[320]{0:T(512)S(1)} %get-tuple-element.232), channel_id=2, replica_groups=mesh['req'=32,'seq'=8] {'seq'}, use_global_device_ids=true, to_apply=%add | all-reduce | flops 320 | bytes 2560
  704.7 46.0 %all-gather.7.cloned.1.call-done = f32[320,64,128]{2,1,0:T(8,128)} async-done(((f32[40,64,128]{2,1,0:T(8,128)}), f32[320,64,128]{2,1,0:T(8,128)}) %all-gather.7.cloned.1.call-update) | async-done | bytes 10485776 | tf_op jit(solution)/shard_map/all_gather | solution.py:25
  750.7 0.1 broadcast.61
  750.8 3.3 while.40
  750.9 1.7 bitcast_add_fusion.4
  752.6 1.6 bitcast_add_fusion.4
  754.2 1.3 add_select_fusion
  755.5 0.3 all-gather.9.cloned.1.call-start
  755.8 74.1 %all-reduce.3.cloned.1.call-done = f32[40,64,128]{2,1,0:T(8,128)} async-done(((f32[40,64,128]{2,1,0:T(8,128)}), f32[40,64,128]{2,1,0:T(8,128)}) %all-reduce.3.cloned.1.call-update) | async-done | bytes 1310736 | tf_op jit(solution)/shard_map/psum | solution.py:38
  829.9 1.6 constant_dynamic-slice_fusion.2
  831.7 0.6 iota_compare_fusion.1
  832.4 8.0 multiply_add_fusion.1
  840.4 8.6 copy.47
  849.1 9.6 %reshape.129 = f32[512,2560]{1,0:T(8,128)} reshape(f32[2,256,40,64]{3,2,1,0:T(8,128)} %copy.47) | data formatting | bytes 10485760 | tf_op jit(solution)/shard_map/reshape | solution.py:138
  858.7 4.4 multiply_reduce_fusion
  863.1 0.4 copy-done.4
  863.5 4.7 fusion.30
  868.2 51.6 %all-gather.9.cloned.1.call-done = f32[160,64,128]{2,1,0:T(8,128)} async-done(((f32[5,64,128]{2,1,0:T(8,128)}), f32[160,64,128]{2,1,0:T(8,128)}) %all-gather.9.cloned.1.call-update) | async-done | bytes 5242896 | tf_op jit(solution)/shard_map/all_gather | solution.py:149
  919.8 3.9 select_reduce_fusion
  (77 shorter events, 1.4 us)
Async XLA Ops:
  7.2 585.8 %copy-start = (bf16[1,512,2560]{2,1,0:T(8,128)(2,1)S(1)}, bf16[1,512,2560]{2,1,0:T(8,128)(2,1)}, u32[]{:S(2)}) copy-start(bf16[1,512,2560]{2,1,0:T(8,128)(2,1)} %param.18) | copy-start | bytes 7864324
  16.1 15.7 %copy-start.12 = (bf16[10,40]{1,0:T(8,128)(2,1)S(1)}, bf16[10,40]{1,0:T(8,128)(2,1)}, u32[]{:S(2)}) copy-start(bf16[10,40]{1,0:T(8,128)(2,1)} %param.20) | copy-start | bytes 2404
  16.1 571.6 %copy-start.14 = (s32[32]{0:T(128)S(1)}, s32[32]{0:T(128)}, u32[]{:S(2)}) copy-start(s32[32]{0:T(128)} %param.29) | copy-start | bytes 388
  16.1 572.3 %copy-start.16 = (s32[32]{0:T(128)S(1)}, s32[32]{0:T(128)}, u32[]{:S(2)}) copy-start(s32[32]{0:T(128)} %param.28) | copy-start | bytes 388
  16.1 573.6 %copy-start.17 = (s32[32]{0:T(128)S(1)}, s32[32]{0:T(128)}, u32[]{:S(2)}) copy-start(s32[32]{0:T(128)} %param.27) | copy-start | bytes 388
  16.1 576.9 %copy-start.13 = (f32[40]{0:T(128)S(1)}, f32[40]{0:T(128)}, u32[]{:S(2)}) copy-start(f32[40]{0:T(128)} %param.23) | copy-start | bytes 484
  16.1 577.8 %all-to-all-start = ((bf16[256,10,2816]{2,1,0:T(8,128)(2,1)}), bf16[256,10,2816]{2,1,0:T(8,128)(2,1)}, u32[]{:S(2)}, u32[]{:S(2)}) async-start(bf16[256,10,2816]{2,1,0:T(8,128)(2,1)} %stack.2), calls=%async_computation | async-start | bytes 46137344 | tf_op jit(solution)/shard_map/all_to_all | solution.py:13
  31.7 719.0 %all-gather.7.cloned.1.call-start = ((), (), s32[]{:S(2)}) async-start(), calls=%async_computation.2 | async-start | bytes 11796480 | tf_op jit(solution)/shard_map/all_gather | solution.py:25
  619.2 15.6 %copy-start.8 = (f32[4,2816]{1,0:T(4,128)S(1)}, f32[4,2816]{1,0:T(4,128)}, u32[]{:S(2)}) copy-start(f32[4,2816]{1,0:T(4,128)} %param.21) | copy-start | bytes 135172
  619.2 21.1 %copy-start.10 = (f32[2816]{0:T(1024)S(1)}, f32[2816]{0:T(1024)}, u32[]{:S(2)}) copy-start(f32[2816]{0:T(1024)} %param.22) | copy-start | bytes 33796
  630.7 1.6 copy-start.7
  632.3 8.0 collective-permute-start
  648.1 1.5 copy-start.5
  658.9 8.2 copy-start.9
  668.3 5.6 copy-start.6
  676.8 5.6 copy-start.6
  686.2 6.8 copy-start.18
  691.8 1.1 copy-start.2
  692.9 137.0 %all-reduce.3.cloned.1.call-start = ((), (), s32[]{:S(2)}) async-start(), calls=%async_computation.1 | async-start | bytes 2621440 | tf_op jit(solution)/shard_map/psum | solution.py:38
  750.8 3.4 copy-start.3
  754.2 77.3 %copy-start.15 = (f32[40]{0:T(128)S(1)}, f32[40]{0:T(128)}, u32[]{:S(2)}) copy-start(f32[40]{0:T(128)} %param.25) | copy-start | bytes 484
  755.5 164.3 %all-gather.9.cloned.1.call-start = ((), (), s32[]{:S(2)}) async-start(), calls=%async_computation.3 | async-start | bytes 5406720 | tf_op jit(solution)/shard_map/all_gather | solution.py:149
  858.7 4.8 copy-start.4
  858.7 4.8 copy-start.11
  863.5 60.1 %copy-start.1 = (bf16[1,512,2560]{2,1,0:T(8,128)(2,1)S(1)}, bf16[1,512,2560]{2,1,0:T(8,128)(2,1)}, u32[]{:S(2)}) copy-start(bf16[1,512,2560]{2,1,0:T(8,128)(2,1)} %param.18) | copy-start | bytes 7864324
Sparse Core Ops, SparseCore 0:
  693.0 57.6 all-gather.6
  755.6 74.2 all-reduce.2
  833.1 86.6 all-gather.8
